TPU v7x, 32 devices: a whole 2x2x4 slice. The times are simulated.
32 devices in a mesh: scene: 8 (over z, y), image: 4 (over x, core).
Axes of the slice: x: 2, y: 2, z: 4, core: 2. Of those that a mesh axis runs over, the one named last changes fastest.
Arguments:
- jacobian: bfloat16 [256, 256, 1152], P(('scene', 'image')), may hold values from -0.1875 to 0.1875
- splat_ids: int32 [256, 128], P(('scene', 'image')), may hold values from 0 to 8191, as said below
- pix_residual: bfloat16 [256, 256], P(('scene', 'image')), may hold values from -6 to 6
- live_blocks: int32 [32], replicated, may hold values from 1 to 8, as said below
- proj_jac: bfloat16 [9, 59, 8192], P(None, None, 'scene'), may hold values from -0.75 to 0.75
- damping: float32 [59, 8192], P(None, 'scene'), may hold values from 0.1 to 1
- precond: float32 [59, 8192], P(None, 'scene'), may hold values from 0.3 to 9
Outputs:
- solution: float32 [59, 8192], P(None, 'scene')
- residual: float32 [59, 8192], P(None, 'scene')
Inputs may be any that keep to these rules, and one draw needn't show every extreme that they name: live_blocks[d] counts the blocks in use on device d = scene index * 4 + image index; they are its slots 0 to live_blocks[d] - 1; some device uses all 8 while the device whose index differs from it in the lowest bit uses at most half of them. `splat_ids`: splat s of every block names a Gaussian of scene index s // 16, that is an id from that index times 1024 to the next such multiple.
All inputs are finite; a program needn't handle non-finite values.
Results may differ from a plain program's by a relative error of at most 0.0051.
Values may be sent and summed in bfloat16 or wider, within the bound.
A program may use at most 64 MiB of HBM per device.

v0:
```python
import jax
import jax.numpy as jnp
from jax import lax
from jax.sharding import PartitionSpec as P

ITERS = 2


def project(proj_jac, field):
    return jnp.einsum(
        "kag,ag->kg", proj_jac.astype(jnp.float32), field, precision=lax.Precision.HIGHEST
    ).astype(jnp.bfloat16)


def lift(proj_jac, weights):
    return jnp.einsum(
        "kag,kg->ag", proj_jac.astype(jnp.float32), weights, precision=lax.Precision.HIGHEST
    )


def run_blocks(jac_set, pixel_set, first_pos, last_pos, picker, keeper, initial):

    def advance(position, running):
        jac_block = lax.dynamic_index_in_dim(jac_set, position, 0, keepdims=False)
        if picker is None:
            signal = lax.dynamic_index_in_dim(pixel_set, position, 0, keepdims=False)
        else:
            signal = jnp.dot(
                jac_block, picker(position), preferred_element_type=jnp.float32
            ).astype(jnp.bfloat16)
        returned = jnp.dot(signal, jac_block, preferred_element_type=jnp.float32)
        return keeper(running, position, returned)

    return lax.fori_loop(first_pos, last_pos, advance, initial)


def local(jacobian, splat_ids, pix_residual, live_blocks, proj_jac, damping, precond):
    g_dev = damping.shape[1]
    n_proj = proj_jac.shape[0]
    n_scene = lax.axis_size("scene")
    owner_width = splat_ids.shape[1] // n_scene
    scene_pos = lax.axis_index("scene")
    device_pos = scene_pos * lax.axis_size("image") + lax.axis_index("image")
    own_live = live_blocks[device_pos]
    block_sets = [(jacobian, splat_ids, pix_residual, 0, own_live)]
    offsets = []
    total_slots = 0
    member = block_sets[0]
    offsets.append(total_slots)
    total_slots += member[0].shape[0]
    ids_all = jnp.concatenate([member[1] for member in block_sets], axis=0)
    routed_ids = lax.all_to_all(
        ids_all.reshape(total_slots, n_scene, owner_width),
        "scene",
        split_axis=1,
        concat_axis=1,
        tiled=True,
    )
    local_ids = routed_ids - scene_pos * g_dev

    def back_project(source):
        buffer = jnp.zeros((total_slots, n_proj, n_scene, owner_width), jnp.float32)
        for index_set, (jac_set, id_set, pixel_set, first_pos, last_pos) in enumerate(block_sets):
            slot_base = offsets[index_set]

            def keeper(running, position, returned):
                shaped = returned.reshape(n_proj, n_scene, owner_width)
                return lax.dynamic_update_index_in_dim(running, shaped, slot_base + position, 0)

            picker = (
                None
                if source is None
                else lambda position: lax.dynamic_index_in_dim(
                    source, slot_base + position, 0, keepdims=False
                )
            )
            buffer = run_blocks(jac_set, pixel_set, first_pos, last_pos, picker, keeper, buffer)
        arrived = lax.all_to_all(buffer, "scene", split_axis=2, concat_axis=2, tiled=True)
        arrivals = jnp.moveaxis(arrived, 1, 0).reshape(n_proj, -1)
        partial_sum = (
            jnp.zeros((n_proj, g_dev), jnp.float32).at[:, local_ids.reshape(-1)].add(arrivals)
        )
        return lax.psum(partial_sum, "image")

    def norm_dot(residual, precon_res):
        return lax.psum(jnp.sum(residual * precon_res), "scene")

    residual = -lift(proj_jac, back_project(None))
    solution = jnp.zeros_like(residual)
    precon_res = precond * residual
    direction = precon_res
    rz_now = norm_dot(residual, precon_res)
    for iteration in range(ITERS):
        local_proj = project(proj_jac, direction)
        picked = jnp.moveaxis(jnp.take(local_proj, local_ids, axis=1), 0, 1)
        fetched = lax.all_to_all(picked, "scene", split_axis=2, concat_axis=2, tiled=True).reshape(
            total_slots, -1
        )
        image = lift(proj_jac, back_project(fetched)) + damping * direction
        alpha = rz_now / lax.psum(jnp.sum(direction * image), "scene")
        solution = solution + alpha * direction
        residual = residual - alpha * image
        precon_res = precond * residual
        rz_next = norm_dot(residual, precon_res)
        direction = precon_res + rz_next / rz_now * direction
        rz_now = rz_next
    return (solution, residual)


def solution(mesh):
    return jax.shard_map(
        local,
        mesh=mesh,
        in_specs=(
            P(("scene", "image"), None, None),
            P(("scene", "image"), None),
            P(("scene", "image"), None),
            P(),
            P(None, None, "scene"),
            P(None, "scene"),
            P(None, "scene"),
        ),
        out_specs=(P(None, "scene"), P(None, "scene")),
        check_vma=False,
    )
```

profile of v0, /device:TPU:0, one launch (start us, length us, event | category | flops | bytes accessed | tf_op | source)
XLA Modules:
  0.0 306.9 jit_solution(1758452299170405827)
XLA Ops:
  2.1 7.3 %all-to-all-start = ((s32[8,1,128]{2,1,0:T(1,128)}), s32[8,1,128]{2,1,0:T(1,128)S(1)}, u32[]{:S(2)}, u32[]{:S(2)}) async-start(s32[8,1,128]{2,1,0:T(1,128)} %reshape.172), calls=%async_computation | async-start | bytes 8192 | tf_op jit(solution)/shard_map/all_to_all | solution.py:52
  9.4 6.6 %copy.58 = bf16[8,256,1152]{1,2,0:T(8,128)(2,1)} copy(bf16[8,256,1152]{2,1,0:T(8,128)(2,1)} %param.15) | data formatting | bytes 9437184 | tf_op jit(solution)/shard_map/while | solution.py:34
  16.6 14.1 %while.30 = (s32[]{:T(128)}, f32[8,9,8,16]{3,0,1,2:T(8,128)S(1)}, s32[]{:T(128)}, bf16[8,256]{1,0:T(8,128)(2,1)}, bf16[8,256,1152]{1,2,0:T(8,128)(2,1)}, /*index=5*/s32[]{:T(128)}, s32[]{:T(128)}, s32[]{:T(128)}) while((s32[]{:T(128)}, f32[8,9,8,16]{3,0,1,2:T(8,128)S(1)}, s32[]{:T(128)}, bf16[8,256]{1,0:T(8,128)(2,1)}, ...), condition=%wide.region_1.2_spmd, body=%wide.region_0.1_spmd.sunk | while | flops 589829 | bytes 1793675 | solution.py:34
  18.3 1.5 fusion.52
  21.7 1.5 fusion.52
  25.1 1.5 fusion.52
  28.5 1.5 fusion.52
  31.5 19.5 %all-to-all-start.1 = ((f32[8,1,1152]{2,1,0:T(1,128)}), f32[8,1,1152]{2,1,0:T(1,128)S(1)}, u32[]{:S(2)}, u32[]{:S(2)}) async-start(f32[8,1,1152]{2,1,0:T(1,128)} %reshape.174), calls=%async_computation.1 | async-start | bytes 73728 | tf_op jit(solution)/shard_map/all_to_all | solution.py:78
  52.5 5.2 %all-to-all-done.1 = f32[8,1,1152]{2,1,0:T(1,128)S(1)} async-done(((f32[8,1,1152]{2,1,0:T(1,128)}), f32[8,1,1152]{2,1,0:T(1,128)S(1)}, u32[]{:S(2)}, u32[]{:S(2)}) %all-to-all-start.1) | async-done | bytes 36896 | tf_op jit(solution)/shard_map/all_to_all | solution.py:78
  59.7 6.2 %scatter_custom_fusion = f32[9,1024]{0,1:T(8,128)S(1)} fusion(s32[1024]{0:T(1024)S(1)} %bitcast.208, f32[1024,9]{1,0:T(8,128)S(1)} %copy.61, f32[]{:T(128)} %constant.63.clone.1), kind=kCustom, calls=%fused_computation.54 | custom fusion | flops 9216 | bytes 36868 | tf_op jit(solution)/shard_map/scatter-add | solution.py:81
  65.9 16.1 %psum.49 = f32[9,1024]{0,1:T(8,128)S(1)} all-reduce(f32[9,1024]{0,1:T(8,128)S(1)} %scatter_custom_fusion), channel_id=1, replica_groups=mesh['scene'=8,'image'=4] {'image'}, use_global_device_ids=true, to_apply=%region_3.4 | all-reduce | flops 9216 | bytes 73728 | tf_op jit(solution)/shard_map/psum | solution.py:83
  83.0 3.2 %gather_fusion = bf16[1024,9]{1,0:T(8,128)(2,1)S(1)} fusion(bf16[9,1024]{0,1:T(8,128)(2,1)S(1)} %bitcast.187, s32[1024]{0:T(1024)S(1)} %broadcast_clamp_fusion), kind=kCustom, calls=%fused_computation.clone | custom fusion | bytes 40960 | tf_op jit(solution)/shard_map/jit(_take)/gather | solution.py:95
  87.5 3.3 %all-to-all-start.2 = ((bf16[8,2,576]{2,1,0:T(2,128)(2,1)}), bf16[8,2,576]{2,1,0:T(2,128)(2,1)S(1)}, u32[]{:S(2)}, u32[]{:S(2)}) async-start(bf16[8,2,576]{2,1,0:T(2,128)(2,1)} %reshape.176), calls=%async_computation.2 | async-start | bytes 40960 | tf_op jit(solution)/shard_map/all_to_all | solution.py:96
  90.8 6.5 %all-to-all-done.2 = bf16[8,2,576]{2,1,0:T(2,128)(2,1)S(1)} async-done(((bf16[8,2,576]{2,1,0:T(2,128)(2,1)}), bf16[8,2,576]{2,1,0:T(2,128)(2,1)S(1)}, u32[]{:S(2)}, u32[]{:S(2)}) %all-to-all-start.2) | async-done | bytes 18464 | tf_op jit(solution)/shard_map/all_to_all | solution.py:96
  97.7 16.5 %while.31 = (s32[]{:T(128)}, f32[8,9,8,16]{3,0,1,2:T(8,128)S(1)}, s32[]{:T(128)}, bf16[8,256,1152]{1,2,0:T(8,128)(2,1)}, bf16[8,1152]{1,0:T(8,128)(2,1)S(1)}, /*index=5*/s32[]{:T(128)}, s32[]{:T(128)}, s32[]{:T(128)}) while((s32[]{:T(128)}, f32[8,9,8,16]{3,0,1,2:T(8,128)S(1)}, s32[]{:T(128)}, bf16[8,256,1152]{1,2,0:T(8,128)(2,1)}, ...), condition=%wide.region_7.9_spmd, body=%wide.region_6.8_spmd.sunk | while | flops 1179909 | bytes 2392199 | solution.py:34
  99.4 1.2 fusion.57
  103.4 1.2 fusion.57
  107.4 1.2 fusion.57
  114.4 24.3 %all_to_all.30 = f32[8,1,1152]{2,1,0:T(1,128)S(1)} all-to-all(f32[8,1,1152]{2,1,0:T(1,128)S(1)} %reshape.178), channel_id=1, replica_groups=mesh['scene'=8,'image'=4] {'scene'}, dimensions={0} | all-to-all | bytes 73728 | tf_op jit(solution)/shard_map/all_to_all | solution.py:78
  140.0 6.2 %scatter_custom_fusion.1 = f32[9,1024]{0,1:T(8,128)S(1)} fusion(s32[1024]{0:T(1024)S(1)} %bitcast.209, f32[1024,9]{1,0:T(8,128)S(1)} %copy.68, f32[]{:T(128)} %constant.63.clone.1), kind=kCustom, calls=%fused_computation.52 | custom fusion | flops 9216 | bytes 36868 | tf_op jit(solution)/shard_map/scatter-add | solution.py:81
  146.2 16.2 %psum.51 = f32[9,1024]{0,1:T(8,128)S(1)} all-reduce(f32[9,1024]{0,1:T(8,128)S(1)} %scatter_custom_fusion.1), channel_id=1, replica_groups=mesh['scene'=8,'image'=4] {'image'}, use_global_device_ids=true, to_apply=%region_9.11 | all-reduce | flops 9216 | bytes 73728 | tf_op jit(solution)/shard_map/psum | solution.py:83
  163.6 18.4 %all-reduce = (f32[]{:T(128)}, f32[]{:T(128)}) all-reduce(f32[]{:T(128)} %get-tuple-element.151, f32[]{:T(128)} %get-tuple-element.150), channel_id=1, replica_groups=mesh['scene'=8,'image'=4] {'scene'}, use_global_device_ids=true, to_apply=%region_5.6 | all-reduce | flops 2 | bytes 16 | tf_op jit(solution)/shard_map/psum | solution.py:86
  183.4 1.4 multiply_reduce_fusion.1
  184.8 19.3 %psum.53 = f32[]{:T(128)} all-reduce(f32[]{:T(128)} %get-tuple-element.184), channel_id=1, replica_groups=mesh['scene'=8,'image'=4] {'scene'}, use_global_device_ids=true, to_apply=%region_13.15 | all-reduce | flops 1 | bytes 8 | tf_op jit(solution)/shard_map/psum | solution.py:86
  206.0 3.2 %gather_fusion.1 = bf16[1024,9]{1,0:T(8,128)(2,1)S(1)} fusion(bf16[9,1024]{0,1:T(8,128)(2,1)S(1)} %bitcast.186, s32[1024]{0:T(1024)S(1)} %broadcast_clamp_fusion), kind=kCustom, calls=%fused_computation.1.clone | custom fusion | bytes 40960 | tf_op jit(solution)/shard_map/jit(_take)/gather | solution.py:95
  210.5 3.3 %all-to-all-start.4 = ((bf16[8,2,576]{2,1,0:T(2,128)(2,1)}), bf16[8,2,576]{2,1,0:T(2,128)(2,1)S(1)}, u32[]{:S(2)}, u32[]{:S(2)}) async-start(bf16[8,2,576]{2,1,0:T(2,128)(2,1)} %reshape.180), calls=%async_computation.4 | async-start | bytes 40960 | tf_op jit(solution)/shard_map/all_to_all | solution.py:96
  213.9 6.5 %all-to-all-done.4 = bf16[8,2,576]{2,1,0:T(2,128)(2,1)S(1)} async-done(((bf16[8,2,576]{2,1,0:T(2,128)(2,1)}), bf16[8,2,576]{2,1,0:T(2,128)(2,1)S(1)}, u32[]{:S(2)}, u32[]{:S(2)}) %all-to-all-start.4) | async-done | bytes 18464 | tf_op jit(solution)/shard_map/all_to_all | solution.py:96
  220.8 16.5 %while.32 = (s32[]{:T(128)}, f32[8,9,8,16]{3,0,1,2:T(8,128)S(1)}, s32[]{:T(128)}, bf16[8,256,1152]{1,2,0:T(8,128)(2,1)}, bf16[8,1152]{1,0:T(8,128)(2,1)S(1)}, /*index=5*/s32[]{:T(128)}, s32[]{:T(128)}, s32[]{:T(128)}) while((s32[]{:T(128)}, f32[8,9,8,16]{3,0,1,2:T(8,128)S(1)}, s32[]{:T(128)}, bf16[8,256,1152]{1,2,0:T(8,128)(2,1)}, ...), condition=%wide.region_15.17_spmd, body=%wide.region_14.16_spmd.sunk | while | flops 1179909 | bytes 2392199 | solution.py:34
  237.4 24.3 %all_to_all.31 = f32[8,1,1152]{2,1,0:T(1,128)S(1)} all-to-all(f32[8,1,1152]{2,1,0:T(1,128)S(1)} %reshape.182), channel_id=1, replica_groups=mesh['scene'=8,'image'=4] {'scene'}, dimensions={0} | all-to-all | bytes 73728 | tf_op jit(solution)/shard_map/all_to_all | solution.py:78
  263.1 6.1 %scatter_custom_fusion.2 = f32[9,1024]{0,1:T(8,128)S(1)} fusion(s32[1024]{0:T(1024)S(1)} %bitcast.210, f32[1024,9]{1,0:T(8,128)S(1)} %copy.75, f32[]{:T(128)} %constant.63.clone.1), kind=kCustom, calls=%fused_computation.50 | custom fusion | flops 9216 | bytes 36868 | tf_op jit(solution)/shard_map/scatter-add | solution.py:81
  269.2 15.8 %psum.54 = f32[9,1024]{0,1:T(8,128)S(1)} all-reduce(f32[9,1024]{0,1:T(8,128)S(1)} %scatter_custom_fusion.2), channel_id=1, replica_groups=mesh['scene'=8,'image'=4] {'image'}, use_global_device_ids=true, to_apply=%region_17.19 | all-reduce | flops 9216 | bytes 73728 | tf_op jit(solution)/shard_map/psum | solution.py:83
  286.2 18.4 %psum.55 = f32[]{:T(128)} all-reduce(f32[]{:T(128)} %multiply_reduce_fusion), channel_id=1, replica_groups=mesh['scene'=8,'image'=4] {'scene'}, use_global_device_ids=true, to_apply=%region_19.21 | all-reduce | flops 1 | bytes 8 | tf_op jit(solution)/shard_map/psum | solution.py:100
  (143 shorter events, 45.7 us)
Async XLA Ops:
  2.1 29.4 %all-to-all-start = ((s32[8,1,128]{2,1,0:T(1,128)}), s32[8,1,128]{2,1,0:T(1,128)S(1)}, u32[]{:S(2)}, u32[]{:S(2)}) async-start(s32[8,1,128]{2,1,0:T(1,128)} %reshape.172), calls=%async_computation | async-start | bytes 8192 | tf_op jit(solution)/shard_map/all_to_all | solution.py:52
  9.4 6.7 %copy-start.4 = (s32[32]{0:T(128)S(1)}, s32[32]{0:T(128)}, u32[]{:S(2)}) copy-start(s32[32]{0:T(128)} %param.18) | copy-start | bytes 388
  31.5 26.3 %all-to-all-start.1 = ((f32[8,1,1152]{2,1,0:T(1,128)}), f32[8,1,1152]{2,1,0:T(1,128)S(1)}, u32[]{:S(2)}, u32[]{:S(2)}) async-start(f32[8,1,1152]{2,1,0:T(1,128)} %reshape.174), calls=%async_computation.1 | async-start | bytes 73728 | tf_op jit(solution)/shard_map/all_to_all | solution.py:78
  52.5 29.6 %copy-start = (bf16[9,59,1024]{2,1,0:T(8,128)(2,1)S(1)}, bf16[9,59,1024]{2,1,0:T(8,128)(2,1)}, u32[]{:S(2)}) copy-start(bf16[9,59,1024]{2,1,0:T(8,128)(2,1)} %param.19) | copy-start | bytes 3262468
  59.3 23.1 %copy-start.2 = (f32[59,1024]{1,0:T(8,128)S(1)}, f32[59,1024]{1,0:T(8,128)}, u32[]{:S(2)}) copy-start(f32[59,1024]{1,0:T(8,128)} %param.21) | copy-start | bytes 724996
  87.5 9.9 %all-to-all-start.2 = ((bf16[8,2,576]{2,1,0:T(2,128)(2,1)}), bf16[8,2,576]{2,1,0:T(2,128)(2,1)S(1)}, u32[]{:S(2)}, u32[]{:S(2)}) async-start(bf16[8,2,576]{2,1,0:T(2,128)(2,1)} %reshape.176), calls=%async_computation.2 | async-start | bytes 40960 | tf_op jit(solution)/shard_map/all_to_all | solution.py:96
  139.6 23.2 %copy-start.1 = (f32[59,1024]{1,0:T(8,128)S(1)}, f32[59,1024]{1,0:T(8,128)}, u32[]{:S(2)}) copy-start(f32[59,1024]{1,0:T(8,128)} %param.20) | copy-start | bytes 724996
  210.5 9.9 %all-to-all-start.4 = ((bf16[8,2,576]{2,1,0:T(2,128)(2,1)}), bf16[8,2,576]{2,1,0:T(2,128)(2,1)S(1)}, u32[]{:S(2)}, u32[]{:S(2)}) async-start(bf16[8,2,576]{2,1,0:T(2,128)(2,1)} %reshape.180), calls=%async_computation.4 | async-start | bytes 40960 | tf_op jit(solution)/shard_map/all_to_all | solution.py:96
  263.1 42.9 %copy-start.3 = (f32[59,1024]{1,0:T(8,128)S(1)}, f32[59,1024]{1,0:T(8,128)}, u32[]{:S(2)}) copy-start(f32[59,1024]{1,0:T(8,128)} %get-tuple-element.186) | copy-start | bytes 724996
where the time goes:
time: 309 us; the launch traced here: 307 us
  blocking collectives  153 us (50%)
  local copies, waits for them, and re-layouts  39.6 us (13%)
  starting transfers between devices  33.5 us (11%)
  other arithmetic  26.5 us (9%)
  matrix products  22.1 us (7%)
  waiting for transfers between devices  18.3 us (6%)
  loops' own time  8.67 us (3%)
  between operations  5.17 us (2%)
    all_to_all x2, blocking collectives, back_project(): lax.all_to_all(buffer, 'scene', split_axis=2, concat_axis=2, tiled=True)  48.6 us
    psum x3, blocking collectives, back_project(): return lax.psum(partial_sum, 'image')  48.2 us
    psum x2, blocking collectives, norm_dot(): return lax.psum(jnp.sum(residual * precon_res), 'scene')  37.7 us
    all_to_all x1, starting transfers between devices, back_project(): lax.all_to_all(buffer, 'scene', split_axis=2, concat_axis=2, tiled=True)  19.5 us
    scatter-add x3, other arithmetic, back_project(): jnp.zeros((n_proj, g_dev), jnp.float32).at[:, local_ids.reshape(-1)]  18.5 us
    psum x1, blocking collectives, local(): alpha = rz_now / lax.psum(jnp.sum(direction * image), 'scene')  18.4 us
    dynamic_slice x12, local copies, waits for them, and re-layouts, advance(): jac_block = lax.dynamic_index_in_dim(jac_set, position, 0, keepdims=False)  13.3 us
    all_to_all x2, waiting for transfers between devices, local(): lax.all_to_all(picked, 'scene', split_axis=2, concat_axis=2, tiled=True)  13.1 us
  transfers between devices with their start and end apart: 4, of which 3 were waited for; matrix products, arithmetic and copies ran while one was open for 7% of the time, Pallas kernels for 0%

commit v1 on v0

v1 whole, which is shorter than its diff:
```python
import functools

import jax
import jax.numpy as jnp
from jax import lax
from jax.experimental import pallas as pl
from jax.experimental.pallas import tpu as pltpu
from jax.sharding import PartitionSpec as P

ITERS = 2
LANES = 128
ROWS = 16
F32 = jnp.float32
BF16 = jnp.bfloat16
MESH = pl.DeviceIdType.MESH


def split3(x):
    hi = x.astype(BF16)
    rest = x - hi.astype(F32)
    mid = rest.astype(BF16)
    low = (rest - mid.astype(F32)).astype(BF16)
    return hi, mid, low


def swap_groups(x, n):
    w = LANES // n
    row = lax.broadcasted_iota(jnp.int32, x.shape, 0)
    lane = lax.broadcasted_iota(jnp.int32, x.shape, 1)
    m = 1
    while m < n:
        row_bit = (row & m) != 0
        lane_bit = (lane & (m * w)) != 0
        up = pltpu.roll(pltpu.roll(x, n - m, 0), w * m, 1)
        down = pltpu.roll(pltpu.roll(x, m, 0), LANES - w * m, 1)
        x = jnp.where(row_bit == lane_bit, x, jnp.where(lane_bit, up, down))
        m *= 2
    return x


def nt(a, b):
    return lax.dot_general(a, b, (((1,), (1,)), ((), ())), preferred_element_type=F32)


def kernel(
    n, n_img,
    live_ref, ids_ref, pix_ref, jac_hbm, proj_hbm, damp_hbm, prec_hbm,
    sol_ref, res_ref,
    jac, proj, damp, prec, hot, direc, ufield,
    id_send, id_recv, back_send, back_recv, gath_send, gath_recv, sum_own, sum_recv,
    load_sem, ssem, rsem, issem, irsem,
):
    n_blk, n_pix, width = jac.shape
    n_proj, n_par, g_dev = proj.shape
    me = lax.axis_index("scene")
    img = lax.axis_index("image")
    device_pos = me * n_img + img

    loads = [pltpu.make_async_copy(jac_hbm.at[b], jac.at[b], load_sem.at[b]) for b in range(n_blk)]
    loads.append(pltpu.make_async_copy(proj_hbm, proj, load_sem.at[n_blk]))
    loads.append(pltpu.make_async_copy(damp_hbm, damp, load_sem.at[n_blk + 1]))
    loads.append(pltpu.make_async_copy(prec_hbm, prec, load_sem.at[n_blk + 2]))
    for load in loads:
        load.start()

    scene_peers = [lax.rem(me + r, n) for r in range(1, n)]
    image_peers = [lax.rem(img + r, n_img) for r in range(1, n_img)]
    barrier = pltpu.get_barrier_semaphore()
    for peer in scene_peers:
        pl.semaphore_signal(barrier, inc=1, device_id={"scene": peer}, device_id_type=MESH)
    for peer in image_peers:
        pl.semaphore_signal(barrier, inc=1, device_id={"image": peer}, device_id_type=MESH)

    live = live_ref[device_pos]
    sends = []

    def exchange(phase, send, recv):
        copies = []
        for r, peer in enumerate(scene_peers):
            copy = pltpu.make_async_remote_copy(
                src_ref=send.at[peer], dst_ref=recv.at[me],
                send_sem=ssem.at[phase, r], recv_sem=rsem.at[phase, r],
                device_id={"scene": peer}, device_id_type=MESH,
            )
            copy.start()
            copies.append(copy)
        recv[me] = send[me]
        sends.extend(copies)
        return copies

    def image_exchange(phase):
        copies = []
        for r, peer in enumerate(image_peers):
            copy = pltpu.make_async_remote_copy(
                src_ref=sum_own.at[phase], dst_ref=sum_recv.at[phase, img],
                send_sem=issem.at[phase, r], recv_sem=irsem.at[phase, r],
                device_id={"image": peer}, device_id_type=MESH,
            )
            copy.start()
            copies.append(copy)
        sum_recv[phase, img] = sum_own[phase]
        sends.extend(copies)
        return copies

    def arrived(copies):
        for copy in copies:
            copy.wait_recv()

    def pad_rows(x, fill):
        if n == n_blk:
            return x
        return jnp.concatenate([x, jnp.full((n - n_blk, LANES), fill, x.dtype)], axis=0)

    block_row = lax.broadcasted_iota(jnp.int32, (n_blk, width), 0)
    pix_row = lax.broadcasted_iota(jnp.int32, (n_blk, n_pix), 0)
    msg_row = lax.broadcasted_iota(jnp.int32, (ROWS, LANES), 0)

    def returned(signals, first):
        total = jnp.zeros((n_blk, width), F32)
        for b in range(n_blk):
            if first:
                loads[b].wait()
            one = jnp.dot(signals, jac[b], preferred_element_type=F32)
            total = jnp.where(block_row == b, one, total)
        return jnp.where(block_row < live, total, 0.0)

    def block_images(vectors):
        total = jnp.zeros((n_blk, n_pix), F32)
        for b in range(n_blk):
            total = jnp.where(pix_row == b, nt(vectors, jac[b]), total)
        return total.astype(BF16)

    def lane_sums(x):
        rows = jnp.sum(x, axis=0, keepdims=True)
        total = rows[:, :LANES]
        for c in range(1, x.shape[1] // LANES):
            total = total + rows[:, c * LANES:(c + 1) * LANES]
        return total

    def send_back(phase, back, extras):
        send, recv = back_send.at[phase], back_recv.at[phase]
        for k in range(n_proj):
            piece = pad_rows(back[:, k * LANES:(k + 1) * LANES], 0.0)
            send[:, k, :] = swap_groups(piece, n)
        for k in range(n_proj, ROWS):
            extra = extras[k - n_proj] if k - n_proj < len(extras) else jnp.zeros((1, LANES), F32)
            send[:, k, :] = jnp.broadcast_to(extra, (n, LANES))
        return exchange(1 + 2 * phase, send, recv)

    def reduce_back(phase, copies):
        arrived(copies)
        recv = back_recv.at[phase]
        arrivals = jnp.concatenate([recv[j] for j in range(n)], axis=1)
        parts = jnp.concatenate(split3(arrivals), axis=0)
        summed = nt(parts, hot[...])
        summed = summed[:ROWS] + summed[ROWS:2 * ROWS] + summed[2 * ROWS:]
        extras = recv[0]
        for j in range(1, n):
            extras = extras + recv[j]
        tail = g_dev + LANES
        sum_own[phase, :, :g_dev] = summed[:8]
        for c in range(g_dev // LANES):
            sum_own[phase, c:c + 1, g_dev:tail] = summed[8:9, c * LANES:(c + 1) * LANES]
        sum_own[phase, :, tail:] = jnp.where(
            msg_row[:8] == 0, extras[n_proj:n_proj + 1], 0.0
        )
        arrived(image_exchange(phase))
        total = sum_recv[phase, 0]
        for i in range(1, n_img):
            total = total + sum_recv[phase, i]
        dot = jnp.sum(total[:, tail:], keepdims=True)
        side = jnp.sum(extras[n_proj + 1:n_proj + 2], keepdims=True)
        return total, dot, side

    def lifted(weights, cols):
        chunk = cols.start // LANES
        total = proj[8, :, cols].astype(F32) * weights[chunk:chunk + 1, g_dev:g_dev + LANES]
        for k in range(8):
            total = total + proj[k, :, cols].astype(F32) * weights[k:k + 1, cols]
        return total

    def chunks():
        return [slice(c * LANES, (c + 1) * LANES) for c in range(g_dev // LANES)]

    def project_chunk(field, cols):
        for k in range(n_proj):
            ufield[k:k + 1, cols] = jnp.sum(
                proj[k, :, cols].astype(F32) * field, axis=0, keepdims=True
            )

    def send_gathered(phase, extras):
        parts = jnp.concatenate(split3(ufield[...]), axis=0)
        picked = jnp.dot(parts, hot[...], preferred_element_type=F32)
        picked = picked[:ROWS] + picked[ROWS:2 * ROWS] + picked[2 * ROWS:]
        send, recv = gath_send.at[phase], gath_recv.at[phase]
        for j in range(n):
            piece = picked[:, j * LANES:(j + 1) * LANES]
            for k, extra in enumerate(extras):
                piece = jnp.where(msg_row == n_proj + k, extra, piece)
            send[j] = piece
        return exchange(2 + 2 * phase, send, recv)

    def take_gathered(phase, copies):
        arrived(copies)
        recv = gath_recv.at[phase]
        pieces = [swap_groups(recv[:, k, :], n)[:n_blk] for k in range(n_proj)]
        extras = recv[0]
        for j in range(1, n):
            extras = extras + recv[j]
        sums = jnp.sum(extras, axis=1, keepdims=True)
        return jnp.concatenate(pieces, axis=1), sums[n_proj:n_proj + 1], sums[n_proj + 1:n_proj + 2]

    routed = swap_groups(pad_rows(ids_ref[...], -1), n)
    id_send[:, 0, :] = routed
    pl.semaphore_wait(barrier, n - 1 + n_img - 1)
    id_copies = exchange(0, id_send, id_recv)

    back = returned(pix_ref[...], True)
    copies = send_back(0, back, [])

    arrived(id_copies)
    ufield[...] = jnp.zeros_like(ufield)
    g_iota = lax.broadcasted_iota(jnp.int32, (g_dev, LANES), 0)
    for j in range(n):
        local_ids = id_recv[j] - me * g_dev
        hot[:, j * LANES:(j + 1) * LANES] = jnp.where(g_iota == local_ids, 1.0, 0.0).astype(BF16)
    for load in loads[n_blk:]:
        load.wait()

    weights, _, _ = reduce_back(0, copies)
    rz_part = jnp.zeros((1, LANES), F32)
    dd_part = jnp.zeros((1, LANES), F32)
    for cols in chunks():
        residual = -lifted(weights, cols)
        res_ref[:, cols] = residual
        z = prec[:, cols] * residual
        direc[:, cols] = z
        rz_part = rz_part + jnp.sum(residual * z, axis=0, keepdims=True)
        dd_part = dd_part + jnp.sum(damp[:, cols] * z * z, axis=0, keepdims=True)
        project_chunk(z, cols)
    copies = send_gathered(0, [rz_part, dd_part])

    vectors = rz_now = None
    for iteration in range(ITERS):
        if iteration == 0:
            vectors, rz_now, dd = take_gathered(0, copies)
            extras = []
        else:
            gathered, rz_next, _ = take_gathered(iteration, copies)
            beta = rz_next / rz_now
            rz_now = rz_next
            vectors = gathered + beta * vectors
            dd_part = jnp.zeros((1, LANES), F32)
            for cols in chunks():
                d = prec[:, cols] * res_ref[:, cols] + beta * direc[:, cols]
                direc[:, cols] = d
                dd_part = dd_part + jnp.sum(damp[:, cols] * d * d, axis=0, keepdims=True)
            extras = [dd_part]
        back = returned(block_images(vectors.astype(BF16)), False)
        copies = send_back(iteration + 1, back, [lane_sums(back * vectors)] + extras)
        weights, dot, side = reduce_back(iteration + 1, copies)
        alpha = rz_now / (dot + (dd if iteration == 0 else side))
        last = iteration == ITERS - 1
        rz_part = jnp.zeros((1, LANES), F32)
        for cols in chunks():
            d = direc[:, cols]
            image = lifted(weights, cols) + damp[:, cols] * d
            residual = res_ref[:, cols] - alpha * image
            res_ref[:, cols] = residual
            sol_ref[:, cols] = alpha * d if iteration == 0 else sol_ref[:, cols] + alpha * d
            if not last:
                z = prec[:, cols] * residual
                rz_part = rz_part + jnp.sum(residual * z, axis=0, keepdims=True)
                project_chunk(z, cols)
        if not last:
            copies = send_gathered(iteration + 1, [rz_part])
    for copy in sends:
        copy.wait_send()


def local(n, n_img, jacobian, splat_ids, pix_residual, live_blocks, proj_jac, damping, precond):
    n_blk, n_pix, width = jacobian.shape
    n_proj, n_par, g_dev = proj_jac.shape
    field = (n_par, g_dev)
    phases = 2 * ITERS + 2
    vmem = pl.BlockSpec(memory_space=pltpu.VMEM)
    hbm = pl.BlockSpec(memory_space=pl.ANY)
    return pl.pallas_call(
        functools.partial(kernel, n, n_img),
        out_shape=[jax.ShapeDtypeStruct(field, F32)] * 2,
        in_specs=[pl.BlockSpec(memory_space=pltpu.SMEM), vmem, vmem, hbm, hbm, hbm, hbm],
        out_specs=[vmem, vmem],
        scratch_shapes=[
            pltpu.VMEM(jacobian.shape, BF16),
            pltpu.VMEM(proj_jac.shape, BF16),
            pltpu.VMEM(field, F32),
            pltpu.VMEM(field, F32),
            pltpu.VMEM((g_dev, n * LANES), BF16),
            pltpu.VMEM(field, F32),
            pltpu.VMEM((ROWS, g_dev), F32),
            pltpu.VMEM((n, 1, LANES), jnp.int32),
            pltpu.VMEM((n, 1, LANES), jnp.int32),
            pltpu.VMEM((ITERS + 1, n, ROWS, LANES), F32),
            pltpu.VMEM((ITERS + 1, n, ROWS, LANES), F32),
            pltpu.VMEM((ITERS, n, ROWS, LANES), F32),
            pltpu.VMEM((ITERS, n, ROWS, LANES), F32),
            pltpu.VMEM((ITERS + 1, 8, g_dev + 2 * LANES), F32),
            pltpu.VMEM((ITERS + 1, n_img, 8, g_dev + 2 * LANES), F32),
            pltpu.SemaphoreType.DMA((n_blk + 3,)),
            pltpu.SemaphoreType.DMA((phases, n - 1)),
            pltpu.SemaphoreType.DMA((phases, n - 1)),
            pltpu.SemaphoreType.DMA((ITERS + 1, n_img - 1)),
            pltpu.SemaphoreType.DMA((ITERS + 1, n_img - 1)),
        ],
        compiler_params=pltpu.CompilerParams(
            collective_id=0, has_side_effects=True, vmem_limit_bytes=50 * 1024 * 1024
        ),
    )(live_blocks, splat_ids, pix_residual, jacobian, proj_jac, damping, precond)


def solution(mesh):
    return jax.shard_map(
        functools.partial(local, mesh.shape["scene"], mesh.shape["image"]),
        mesh=mesh,
        in_specs=(
            P(("scene", "image"), None, None),
            P(("scene", "image"), None),
            P(("scene", "image"), None),
            P(),
            P(None, None, "scene"),
            P(None, "scene"),
            P(None, "scene"),
        ),
        out_specs=(P(None, "scene"), P(None, "scene")),
        check_vma=False,
    )
```

time: 309 us -> 56.4 us (0.18)
  blocking collectives: 153 us -> 0 us
  Pallas kernels: 0 us -> 48.9 us
  starting transfers between devices: 33.5 us -> 0 us
  local copies, waits for them, and re-layouts: 39.6 us -> 6.6 us
  other arithmetic: 26.5 us -> 0 us
  matrix products: 22.1 us -> 0 us
  waiting for transfers between devices: 18.3 us -> 0 us
  loops' own time: 8.67 us -> 0 us
  between operations: 5.17 us -> 0.65 us
    psum x6 -> x0, blocking collectives: 104 us -> none  [the longest x3 48.2 us: back_project(): return lax.psum(partial_sum, 'image')]
    pallas_call x0 -> x1, Pallas kernels: none -> 48.9 us  [local(): pl.pallas_call(functools.partial(kernel, n, n_img), out_shape=[jax.ShapeD...]
    all_to_all x2 -> x0, blocking collectives: 48.6 us -> none  [back_project(): lax.all_to_all(buffer, 'scene', split_axis=2, concat_axis=2, tiled=True)]
    all_to_all x4 -> x0, starting transfers between devices: 33.5 us -> none  [the longest x1 19.5 us: back_project(): lax.all_to_all(buffer, 'scene', split_axis=2, concat_axis=2, tiled=True)]
    dot_general x20 -> x0, matrix products: 22.1 us -> none  [the longest x12 12.2 us: advance(): returned = jnp.dot(signal, jac_block, preferred_element_type=jnp.float32)]
    scatter-add x3 -> x0, other arithmetic: 18.5 us -> none  [back_project(): jnp.zeros((n_proj, g_dev), jnp.float32).at[:, local_ids.reshape(-1)]]
    all_to_all x4 -> x0, waiting for transfers between devices: 18.3 us -> none  [the longest x2 13.1 us: local(): lax.all_to_all(picked, 'scene', split_axis=2, concat_axis=2, tiled=True)]
    dynamic_slice x13 -> x0, local copies, waits for them, and re-layouts: 13.9 us -> none  [the longest x12 13.3 us: advance(): jac_block = lax.dynamic_index_in_dim(jac_set, position, 0, keepdims=False)]
  transfers between devices with their start and end apart: 4 -> 0, of which waited for: 3 -> 0; matrix products, arithmetic and copies ran while one was open for 7% -> 0% of each run, Pallas kernels for 0% -> 0%
where the time goes in v1:
time: 56.4 us; the launch traced here: 56.1 us
  Pallas kernels  48.9 us (87%)
  local copies, waits for them, and re-layouts  6.6 us (12%)
  between operations  0.65 us (1%)
    pallas_call x1, Pallas kernels, local(): pl.pallas_call(functools.partial(kernel, n, n_img), out_shape=[jax.ShapeD...  48.9 us
    unnamed x14, local copies, waits for them, and re-layouts  6.6 us

profile of v1, /device:TPU:0, one launch (start us, length us, event | category | flops | bytes accessed | tf_op | source)
XLA Modules:
  0.0 56.1 jit_solution(16447806351444890717)
XLA Ops:
  0.6 0.0 copy-start
  0.6 1.3 %copy-done = bf16[9,59,1024]{2,1,0:T(8,128)(2,1)S(1)} copy-done((bf16[9,59,1024]{2,1,0:T(8,128)(2,1)S(1)}, bf16[9,59,1024]{2,1,0:T(8,128)(2,1)}, u32[]{:S(2)}) %copy-start) | copy-done | bytes 1087512
  1.9 0.0 copy-start.1
  1.9 0.9 %copy-done.1 = f32[59,1024]{1,0:T(8,128)S(1)} copy-done((f32[59,1024]{1,0:T(8,128)S(1)}, f32[59,1024]{1,0:T(8,128)}, u32[]{:S(2)}) %copy-start.1) | copy-done | bytes 241688
  2.9 0.0 copy-start.2
  2.9 0.9 %copy-done.2 = f32[59,1024]{1,0:T(8,128)S(1)} copy-done((f32[59,1024]{1,0:T(8,128)S(1)}, f32[59,1024]{1,0:T(8,128)}, u32[]{:S(2)}) %copy-start.2) | copy-done | bytes 241688
  3.8 0.0 copy-start.3
  3.8 0.7 %copy-done.3 = s32[8,128]{1,0:T(8,128)S(1)} copy-done((s32[8,128]{1,0:T(8,128)S(1)}, s32[8,128]{1,0:T(8,128)}, u32[]{:S(2)}) %copy-start.3) | copy-done | bytes 4120
  4.5 0.0 copy-start.4
  4.5 0.7 %copy-done.4 = bf16[8,256]{1,0:T(8,128)(2,1)S(1)} copy-done((bf16[8,256]{1,0:T(8,128)(2,1)S(1)}, bf16[8,256]{1,0:T(8,128)(2,1)}, u32[]{:S(2)}) %copy-start.4) | copy-done | bytes 4120
  5.2 0.0 copy-start.5
  5.2 0.7 %copy-done.5 = s32[32]{0:T(128)S(1)} copy-done((s32[32]{0:T(128)S(1)}, s32[32]{0:T(128)}, u32[]{:S(2)}) %copy-start.5) | copy-done | bytes 152
  5.8 48.9 %shard_map.86 = (f32[59,1024]{1,0:T(8,128)S(1)}, f32[59,1024]{1,0:T(8,128)S(1)}) custom-call(s32[32]{0:T(128)S(1)} %copy-done.5, s32[8,128]{1,0:T(8,128)S(1)} %copy-done.3, bf16[8,256]{1,0:T(8,128)(2,1)S(1)} %copy-done.4, bf16[8,256,1152]{2,1,0:T(8,128)(2,1)} %jac_hbm.1, bf16[9,59,1024]{2,1,0:T(8,128)(2,1)S(1)} %copy-done, f32[59,1024]{1,0:T(8,128)S(1)} %copy-done.1, ...), custom_call_target="tpu_custom_call" | custom-call | tf_op jit(solution)/shard_map/pallas_call | solution.py:288
  54.7 0.7 %copy.11 = f32[59,1024]{1,0:T(8,128)} copy(f32[59,1024]{1,0:T(8,128)S(1)} %get-tuple-element.4) | data formatting | bytes 483328
  55.4 0.7 %copy.12 = f32[59,1024]{1,0:T(8,128)} copy(f32[59,1024]{1,0:T(8,128)S(1)} %get-tuple-element.5) | data formatting | bytes 483328
Async XLA Ops:
  0.6 1.3 %copy-start = (bf16[9,59,1024]{2,1,0:T(8,128)(2,1)S(1)}, bf16[9,59,1024]{2,1,0:T(8,128)(2,1)}, u32[]{:S(2)}) copy-start(bf16[9,59,1024]{2,1,0:T(8,128)(2,1)} %proj_hbm.1) | copy-start | bytes 3262468
  1.9 0.9 %copy-start.1 = (f32[59,1024]{1,0:T(8,128)S(1)}, f32[59,1024]{1,0:T(8,128)}, u32[]{:S(2)}) copy-start(f32[59,1024]{1,0:T(8,128)} %damp_hbm.1) | copy-start | bytes 724996
  2.9 0.9 %copy-start.2 = (f32[59,1024]{1,0:T(8,128)S(1)}, f32[59,1024]{1,0:T(8,128)}, u32[]{:S(2)}) copy-start(f32[59,1024]{1,0:T(8,128)} %prec_hbm.1) | copy-start | bytes 724996
  3.8 0.7 %copy-start.3 = (s32[8,128]{1,0:T(8,128)S(1)}, s32[8,128]{1,0:T(8,128)}, u32[]{:S(2)}) copy-start(s32[8,128]{1,0:T(8,128)} %ids_ref.1) | copy-start | bytes 12292
  4.5 0.7 %copy-start.4 = (bf16[8,256]{1,0:T(8,128)(2,1)S(1)}, bf16[8,256]{1,0:T(8,128)(2,1)}, u32[]{:S(2)}) copy-start(bf16[8,256]{1,0:T(8,128)(2,1)} %pix_ref.1) | copy-start | bytes 12292
  5.2 0.7 %copy-start.5 = (s32[32]{0:T(128)S(1)}, s32[32]{0:T(128)}, u32[]{:S(2)}) copy-start(s32[32]{0:T(128)} %live_ref.1) | copy-start | bytes 388

commit v2 on v1

--- a/solution.py
+++ b/solution.py
@@ -44,9 +44,9 @@
 
 def kernel(
     n, n_img,
-    live_ref, ids_ref, pix_ref, jac_hbm, proj_hbm, damp_hbm, prec_hbm,
+    live_hbm, ids_hbm, pix_hbm, jac_hbm, proj_hbm, damp_hbm, prec_hbm,
     sol_ref, res_ref,
-    jac, proj, damp, prec, hot, direc, ufield,
+    live_ref, ids_ref, pix_ref, jac, proj, damp, prec, hot, direc, ufield,
     id_send, id_recv, back_send, back_recv, gath_send, gath_recv, sum_own, sum_recv,
     load_sem, ssem, rsem, issem, irsem,
 ):
@@ -56,6 +56,14 @@
     img = lax.axis_index("image")
     device_pos = me * n_img + img
 
+    small = [
+        pltpu.make_async_copy(src, dst, load_sem.at[n_blk + 3 + i])
+        for i, (src, dst) in enumerate(
+            [(ids_hbm, ids_ref), (pix_hbm, pix_ref), (live_hbm, live_ref)]
+        )
+    ]
+    for load in small:
+        load.start()
     loads = [pltpu.make_async_copy(jac_hbm.at[b], jac.at[b], load_sem.at[b]) for b in range(n_blk)]
     loads.append(pltpu.make_async_copy(proj_hbm, proj, load_sem.at[n_blk]))
     loads.append(pltpu.make_async_copy(damp_hbm, damp, load_sem.at[n_blk + 1]))
@@ -71,6 +79,8 @@
     for peer in image_peers:
         pl.semaphore_signal(barrier, inc=1, device_id={"image": peer}, device_id_type=MESH)
 
+    for load in small:
+        load.wait()
     live = live_ref[device_pos]
     sends = []
 
@@ -288,9 +298,12 @@
     return pl.pallas_call(
         functools.partial(kernel, n, n_img),
         out_shape=[jax.ShapeDtypeStruct(field, F32)] * 2,
-        in_specs=[pl.BlockSpec(memory_space=pltpu.SMEM), vmem, vmem, hbm, hbm, hbm, hbm],
+        in_specs=[hbm] * 7,
         out_specs=[vmem, vmem],
         scratch_shapes=[
+            pltpu.SMEM(live_blocks.shape, jnp.int32),
+            pltpu.VMEM(splat_ids.shape, jnp.int32),
+            pltpu.VMEM(pix_residual.shape, BF16),
             pltpu.VMEM(jacobian.shape, BF16),
             pltpu.VMEM(proj_jac.shape, BF16),
             pltpu.VMEM(field, F32),
@@ -306,14 +319,14 @@
             pltpu.VMEM((ITERS, n, ROWS, LANES), F32),
             pltpu.VMEM((ITERS + 1, 8, g_dev + 2 * LANES), F32),
             pltpu.VMEM((ITERS + 1, n_img, 8, g_dev + 2 * LANES), F32),
-            pltpu.SemaphoreType.DMA((n_blk + 3,)),
+            pltpu.SemaphoreType.DMA((n_blk + 6,)),
             pltpu.SemaphoreType.DMA((phases, n - 1)),
             pltpu.SemaphoreType.DMA((phases, n - 1)),
             pltpu.SemaphoreType.DMA((ITERS + 1, n_img - 1)),
             pltpu.SemaphoreType.DMA((ITERS + 1, n_img - 1)),
         ],
         compiler_params=pltpu.CompilerParams(
-            collective_id=0, has_side_effects=True, vmem_limit_bytes=50 * 1024 * 1024
+            collective_id=0, has_side_effects=True, vmem_limit_bytes=67043328
         ),
     )(live_blocks, splat_ids, pix_residual, jacobian, proj_jac, damping, precond)
 

time: 56.4 us -> 53.1 us (0.941)
  local copies, waits for them, and re-layouts: 6.6 us -> 3.34 us
    unnamed x14 -> x2, local copies, waits for them, and re-layouts: 6.6 us -> 3.34 us
where the time goes in v2:
time: 53.1 us; the launch traced here: 52.9 us
  Pallas kernels  48.9 us (92%)
  local copies, waits for them, and re-layouts  3.34 us (6%)
  between operations  0.64 us (1%)
    pallas_call x1, Pallas kernels, local(): pl.pallas_call(functools.partial(kernel, n, n_img), out_shape=[jax.ShapeD...  48.9 us
    unnamed x2, local copies, waits for them, and re-layouts  3.34 us

profile of v2, /device:TPU:0, one launch (start us, length us, event | category | flops | bytes accessed | tf_op | source)
XLA Modules:
  0.0 52.9 jit_solution(4552526216455476306)
XLA Ops:
  0.6 48.9 %shard_map.86 = (f32[59,1024]{1,0:T(8,128)}, f32[59,1024]{1,0:T(8,128)}) custom-call(s32[32]{0:T(128)} %live_hbm.1, s32[8,128]{1,0:T(8,128)} %ids_hbm.1, bf16[8,256]{1,0:T(8,128)(2,1)} %pix_hbm.1, bf16[8,256,1152]{2,1,0:T(8,128)(2,1)} %jac_hbm.1, bf16[9,59,1024]{2,1,0:T(8,128)(2,1)} %proj_hbm.1, f32[59,1024]{1,0:T(8,128)} %damp_hbm.1, f32[59,1024]{1,0:T(8,128)} %prec_hbm.1), custom_call_target="tpu_custom_call" | custom-call | tf_op jit(solution)/shard_map/pallas_call | solution.py:298
  49.6 1.7 %copy.11 = f32[59,1024]{1,0:T(8,128)} copy(f32[59,1024]{1,0:T(8,128)} %get-tuple-element.4) | data formatting | bytes 483328
  51.2 1.7 %copy.12 = f32[59,1024]{1,0:T(8,128)} copy(f32[59,1024]{1,0:T(8,128)} %get-tuple-element.5) | data formatting | bytes 483328

commit v3 on v2

--- a/solution.py
+++ b/solution.py
@@ -84,37 +84,50 @@
     live = live_ref[device_pos]
     sends = []
 
+    def remote(phase, send, recv, peer, r):
+        return pltpu.make_async_remote_copy(
+            src_ref=send.at[peer], dst_ref=recv.at[me],
+            send_sem=ssem.at[phase, r], recv_sem=rsem.at[phase, me],
+            device_id={"scene": peer}, device_id_type=MESH,
+        )
+
     def exchange(phase, send, recv):
-        copies = []
         for r, peer in enumerate(scene_peers):
-            copy = pltpu.make_async_remote_copy(
-                src_ref=send.at[peer], dst_ref=recv.at[me],
-                send_sem=ssem.at[phase, r], recv_sem=rsem.at[phase, r],
-                device_id={"scene": peer}, device_id_type=MESH,
-            )
+            copy = remote(phase, send, recv, peer, r)
             copy.start()
-            copies.append(copy)
+            sends.append(copy)
         recv[me] = send[me]
-        sends.extend(copies)
-        return copies
-
-    def image_exchange(phase):
+
+    def wait_from(phase, recv, source):
+        pltpu.make_async_remote_copy(
+            src_ref=recv.at[source], dst_ref=recv.at[source],
+            send_sem=ssem.at[phase, 0], recv_sem=rsem.at[phase, source],
+            device_id={"scene": source}, device_id_type=MESH,
+        ).wait_recv()
+
+    def wait_all(phase, recv):
+        for peer in scene_peers:
+            wait_from(phase, recv, peer)
+
+    n_pairs = n // 2
+    pair_order = sorted(range(n_pairs), key=lambda o: min(o, n_pairs - o))
+    pairs = [lax.rem(me // 2 + o, n_pairs) for o in pair_order]
+    partner = me + 1 - 2 * lax.rem(me, 2)
+    half = g_dev // 2
+
+    def image_exchange(phase, h):
         copies = []
         for r, peer in enumerate(image_peers):
             copy = pltpu.make_async_remote_copy(
-                src_ref=sum_own.at[phase], dst_ref=sum_recv.at[phase, img],
-                send_sem=issem.at[phase, r], recv_sem=irsem.at[phase, r],
+                src_ref=sum_own.at[phase, h], dst_ref=sum_recv.at[phase, h, img],
+                send_sem=issem.at[phase, h, r], recv_sem=irsem.at[phase, h, r],
                 device_id={"image": peer}, device_id_type=MESH,
             )
             copy.start()
             copies.append(copy)
-        sum_recv[phase, img] = sum_own[phase]
+        sum_recv[phase, h, img] = sum_own[phase, h]
         sends.extend(copies)
         return copies
-
-    def arrived(copies):
-        for copy in copies:
-            copy.wait_recv()
 
     def pad_rows(x, fill):
         if n == n_blk:
@@ -155,42 +168,60 @@
         for k in range(n_proj, ROWS):
             extra = extras[k - n_proj] if k - n_proj < len(extras) else jnp.zeros((1, LANES), F32)
             send[:, k, :] = jnp.broadcast_to(extra, (n, LANES))
-        return exchange(1 + 2 * phase, send, recv)
-
-    def reduce_back(phase, copies):
-        arrived(copies)
+        exchange(1 + 2 * phase, send, recv)
+
+    def start_reduce(phase):
         recv = back_recv.at[phase]
-        arrivals = jnp.concatenate([recv[j] for j in range(n)], axis=1)
-        parts = jnp.concatenate(split3(arrivals), axis=0)
-        summed = nt(parts, hot[...])
-        summed = summed[:ROWS] + summed[ROWS:2 * ROWS] + summed[2 * ROWS:]
+        sums = [None, None]
+        started = []
+        for order, pair in enumerate(pairs):
+            low = 2 * pair
+            if order == 0:
+                wait_from(1 + 2 * phase, recv, partner)
+            else:
+                wait_from(1 + 2 * phase, recv, low)
+                wait_from(1 + 2 * phase, recv, low + 1)
+            arrivals = jnp.concatenate([recv[low], recv[low + 1]], axis=1)
+            parts = jnp.concatenate(split3(arrivals), axis=0)
+            lanes = pl.ds(pl.multiple_of(pair * (2 * LANES), 2 * LANES), 2 * LANES)
+            for h in range(2):
+                one = nt(parts, hot[h * half:(h + 1) * half, lanes])
+                sums[h] = one if order == 0 else sums[h] + one
         extras = recv[0]
         for j in range(1, n):
             extras = extras + recv[j]
-        tail = g_dev + LANES
-        sum_own[phase, :, :g_dev] = summed[:8]
-        for c in range(g_dev // LANES):
-            sum_own[phase, c:c + 1, g_dev:tail] = summed[8:9, c * LANES:(c + 1) * LANES]
-        sum_own[phase, :, tail:] = jnp.where(
-            msg_row[:8] == 0, extras[n_proj:n_proj + 1], 0.0
-        )
-        arrived(image_exchange(phase))
-        total = sum_recv[phase, 0]
+        for h in range(2):
+            summed = sums[h]
+            summed = summed[:ROWS] + summed[ROWS:2 * ROWS] + summed[2 * ROWS:]
+            sum_own[phase, h, :, :half] = summed[:8]
+            sum_own[phase, h, :, half:] = jnp.where(
+                msg_row[:8] == 7, extras[n_proj:n_proj + 1], 0.0
+            )
+            for c in range(half // LANES):
+                sum_own[phase, h, c:c + 1, half:] = summed[8:9, c * LANES:(c + 1) * LANES]
+            started.append(image_exchange(phase, h))
+        side = jnp.sum(extras[n_proj + 1:n_proj + 2], keepdims=True)
+        return started, side
+
+    def finish_reduce(phase, h, copies):
+        for copy in copies:
+            copy.wait_recv()
+        total = sum_recv[phase, h, 0]
         for i in range(1, n_img):
-            total = total + sum_recv[phase, i]
-        dot = jnp.sum(total[:, tail:], keepdims=True)
-        side = jnp.sum(extras[n_proj + 1:n_proj + 2], keepdims=True)
-        return total, dot, side
+            total = total + sum_recv[phase, h, i]
+        return total
 
     def lifted(weights, cols):
-        chunk = cols.start // LANES
-        total = proj[8, :, cols].astype(F32) * weights[chunk:chunk + 1, g_dev:g_dev + LANES]
+        here = cols.start % half
+        chunk = here // LANES
+        total = proj[8, :, cols].astype(F32) * weights[chunk:chunk + 1, half:]
         for k in range(8):
-            total = total + proj[k, :, cols].astype(F32) * weights[k:k + 1, cols]
+            total = total + proj[k, :, cols].astype(F32) * weights[k:k + 1, here:here + LANES]
         return total
 
-    def chunks():
-        return [slice(c * LANES, (c + 1) * LANES) for c in range(g_dev // LANES)]
+    def chunks(h=None):
+        first, last = (0, g_dev) if h is None else (h * half, (h + 1) * half)
+        return [slice(c, c + LANES) for c in range(first, last, LANES)]
 
     def project_chunk(field, cols):
         for k in range(n_proj):
@@ -200,19 +231,28 @@
 
     def send_gathered(phase, extras):
         parts = jnp.concatenate(split3(ufield[...]), axis=0)
-        picked = jnp.dot(parts, hot[...], preferred_element_type=F32)
-        picked = picked[:ROWS] + picked[ROWS:2 * ROWS] + picked[2 * ROWS:]
         send, recv = gath_send.at[phase], gath_recv.at[phase]
-        for j in range(n):
-            piece = picked[:, j * LANES:(j + 1) * LANES]
-            for k, extra in enumerate(extras):
-                piece = jnp.where(msg_row == n_proj + k, extra, piece)
-            send[j] = piece
-        return exchange(2 + 2 * phase, send, recv)
-
-    def take_gathered(phase, copies):
-        arrived(copies)
+        for order in reversed(range(n_pairs)):
+            low = 2 * pairs[order]
+            lanes = pl.ds(pl.multiple_of(pairs[order] * (2 * LANES), 2 * LANES), 2 * LANES)
+            picked = jnp.dot(parts, hot[:, lanes], preferred_element_type=F32)
+            picked = picked[:ROWS] + picked[ROWS:2 * ROWS] + picked[2 * ROWS:]
+            for e in range(2):
+                piece = picked[:, e * LANES:(e + 1) * LANES]
+                for k, extra in enumerate(extras):
+                    piece = jnp.where(msg_row == n_proj + k, extra, piece)
+                send[low + e] = piece
+            targets = [partner] if order == 0 else [low, low + 1]
+            for e, target in enumerate(targets):
+                r = 0 if order == 0 else 2 * order - 1 + e
+                copy = remote(2 + 2 * phase, send, recv, target, r)
+                copy.start()
+                sends.append(copy)
+        recv[me] = send[me]
+
+    def take_gathered(phase):
         recv = gath_recv.at[phase]
+        wait_all(2 + 2 * phase, recv)
         pieces = [swap_groups(recv[:, k, :], n)[:n_blk] for k in range(n_proj)]
         extras = recv[0]
         for j in range(1, n):
@@ -223,12 +263,12 @@
     routed = swap_groups(pad_rows(ids_ref[...], -1), n)
     id_send[:, 0, :] = routed
     pl.semaphore_wait(barrier, n - 1 + n_img - 1)
-    id_copies = exchange(0, id_send, id_recv)
+    exchange(0, id_send, id_recv)
 
     back = returned(pix_ref[...], True)
-    copies = send_back(0, back, [])
-
-    arrived(id_copies)
+    send_back(0, back, [])
+
+    wait_all(0, id_recv)
     ufield[...] = jnp.zeros_like(ufield)
     g_iota = lax.broadcasted_iota(jnp.int32, (g_dev, LANES), 0)
     for j in range(n):
@@ -237,53 +277,60 @@
     for load in loads[n_blk:]:
         load.wait()
 
-    weights, _, _ = reduce_back(0, copies)
+    started, _ = start_reduce(0)
     rz_part = jnp.zeros((1, LANES), F32)
     dd_part = jnp.zeros((1, LANES), F32)
-    for cols in chunks():
-        residual = -lifted(weights, cols)
-        res_ref[:, cols] = residual
-        z = prec[:, cols] * residual
-        direc[:, cols] = z
-        rz_part = rz_part + jnp.sum(residual * z, axis=0, keepdims=True)
-        dd_part = dd_part + jnp.sum(damp[:, cols] * z * z, axis=0, keepdims=True)
-        project_chunk(z, cols)
-    copies = send_gathered(0, [rz_part, dd_part])
+    for h in range(2):
+        weights = finish_reduce(0, h, started[h])
+        for cols in chunks(h):
+            residual = -lifted(weights, cols)
+            res_ref[:, cols] = residual
+            z = prec[:, cols] * residual
+            direc[:, cols] = z
+            rz_part = rz_part + jnp.sum(residual * z, axis=0, keepdims=True)
+            dd_part = dd_part + jnp.sum(damp[:, cols] * z * z, axis=0, keepdims=True)
+            project_chunk(z, cols)
+    send_gathered(0, [rz_part, dd_part])
 
     vectors = rz_now = None
     for iteration in range(ITERS):
         if iteration == 0:
-            vectors, rz_now, dd = take_gathered(0, copies)
-            extras = []
+            vectors, rz_now, dd = take_gathered(0)
         else:
-            gathered, rz_next, _ = take_gathered(iteration, copies)
+            gathered, rz_next, _ = take_gathered(iteration)
             beta = rz_next / rz_now
             rz_now = rz_next
             vectors = gathered + beta * vectors
+        back = returned(block_images(vectors.astype(BF16)), False)
+        extras = []
+        if iteration > 0:
             dd_part = jnp.zeros((1, LANES), F32)
             for cols in chunks():
                 d = prec[:, cols] * res_ref[:, cols] + beta * direc[:, cols]
                 direc[:, cols] = d
                 dd_part = dd_part + jnp.sum(damp[:, cols] * d * d, axis=0, keepdims=True)
             extras = [dd_part]
-        back = returned(block_images(vectors.astype(BF16)), False)
-        copies = send_back(iteration + 1, back, [lane_sums(back * vectors)] + extras)
-        weights, dot, side = reduce_back(iteration + 1, copies)
-        alpha = rz_now / (dot + (dd if iteration == 0 else side))
+        send_back(iteration + 1, back, [lane_sums(back * vectors)] + extras)
+        started, side = start_reduce(iteration + 1)
         last = iteration == ITERS - 1
         rz_part = jnp.zeros((1, LANES), F32)
-        for cols in chunks():
-            d = direc[:, cols]
-            image = lifted(weights, cols) + damp[:, cols] * d
-            residual = res_ref[:, cols] - alpha * image
-            res_ref[:, cols] = residual
-            sol_ref[:, cols] = alpha * d if iteration == 0 else sol_ref[:, cols] + alpha * d
-            if not last:
-                z = prec[:, cols] * residual
-                rz_part = rz_part + jnp.sum(residual * z, axis=0, keepdims=True)
-                project_chunk(z, cols)
+        for h in range(2):
+            weights = finish_reduce(iteration + 1, h, started[h])
+            if h == 0:
+                dot = jnp.sum(weights[7:8, half:], keepdims=True)
+                alpha = rz_now / (dot + (dd if iteration == 0 else side))
+            for cols in chunks(h):
+                d = direc[:, cols]
+                image = lifted(weights, cols) + damp[:, cols] * d
+                residual = res_ref[:, cols] - alpha * image
+                res_ref[:, cols] = residual
+                sol_ref[:, cols] = alpha * d if iteration == 0 else sol_ref[:, cols] + alpha * d
+                if not last:
+                    z = prec[:, cols] * residual
+                    rz_part = rz_part + jnp.sum(residual * z, axis=0, keepdims=True)
+                    project_chunk(z, cols)
         if not last:
-            copies = send_gathered(iteration + 1, [rz_part])
+            send_gathered(iteration + 1, [rz_part])
     for copy in sends:
         copy.wait_send()
 
@@ -294,7 +341,7 @@
     field = (n_par, g_dev)
     phases = 2 * ITERS + 2
     vmem = pl.BlockSpec(memory_space=pltpu.VMEM)
-    hbm = pl.BlockSpec(memory_space=pl.ANY)
+    hbm = pl.BlockSpec(memory_space=pltpu.HBM)
     return pl.pallas_call(
         functools.partial(kernel, n, n_img),
         out_shape=[jax.ShapeDtypeStruct(field, F32)] * 2,
@@ -317,13 +364,13 @@
             pltpu.VMEM((ITERS + 1, n, ROWS, LANES), F32),
             pltpu.VMEM((ITERS, n, ROWS, LANES), F32),
             pltpu.VMEM((ITERS, n, ROWS, LANES), F32),
-            pltpu.VMEM((ITERS + 1, 8, g_dev + 2 * LANES), F32),
-            pltpu.VMEM((ITERS + 1, n_img, 8, g_dev + 2 * LANES), F32),
+            pltpu.VMEM((ITERS + 1, 2, 8, g_dev // 2 + LANES), F32),
+            pltpu.VMEM((ITERS + 1, 2, n_img, 8, g_dev // 2 + LANES), F32),
             pltpu.SemaphoreType.DMA((n_blk + 6,)),
             pltpu.SemaphoreType.DMA((phases, n - 1)),
-            pltpu.SemaphoreType.DMA((phases, n - 1)),
-            pltpu.SemaphoreType.DMA((ITERS + 1, n_img - 1)),
-            pltpu.SemaphoreType.DMA((ITERS + 1, n_img - 1)),
+            pltpu.SemaphoreType.DMA((phases, n)),
+            pltpu.SemaphoreType.DMA((ITERS + 1, 2, n_img - 1)),
+            pltpu.SemaphoreType.DMA((ITERS + 1, 2, n_img - 1)),
         ],
         compiler_params=pltpu.CompilerParams(
             collective_id=0, has_side_effects=True, vmem_limit_bytes=67043328

time: 53.1 us -> 52.8 us (level)
  no operation moved by 1% of the time
where the time goes in v3:
time: 52.8 us; the launch traced here: 52.6 us
  Pallas kernels  48.6 us (92%)
  local copies, waits for them, and re-layouts  3.34 us (6%)
  between operations  0.64 us (1%)
    pallas_call x1, Pallas kernels, local(): pl.pallas_call(functools.partial(kernel, n, n_img), out_shape=[jax.ShapeD...  48.6 us
    unnamed x2, local copies, waits for them, and re-layouts  3.34 us

profile of v3, /device:TPU:0, one launch (start us, length us, event | category | flops | bytes accessed | tf_op | source)
XLA Modules:
  0.0 52.6 jit_solution(4017496749085117283)
XLA Ops:
  0.6 48.6 %shard_map.86 = (f32[59,1024]{1,0:T(8,128)}, f32[59,1024]{1,0:T(8,128)}) custom-call(s32[32]{0:T(128)} %live_hbm.1, s32[8,128]{1,0:T(8,128)} %ids_hbm.1, bf16[8,256]{1,0:T(8,128)(2,1)} %pix_hbm.1, bf16[8,256,1152]{2,1,0:T(8,128)(2,1)} %jac_hbm.1, bf16[9,59,1024]{2,1,0:T(8,128)(2,1)} %proj_hbm.1, f32[59,1024]{1,0:T(8,128)} %damp_hbm.1, f32[59,1024]{1,0:T(8,128)} %prec_hbm.1), custom_call_target="tpu_custom_call" | custom-call | tf_op jit(solution)/shard_map/pallas_call | solution.py:345
  49.3 1.7 %copy.11 = f32[59,1024]{1,0:T(8,128)} copy(f32[59,1024]{1,0:T(8,128)} %get-tuple-element.4) | data formatting | bytes 483328
  50.9 1.7 %copy.12 = f32[59,1024]{1,0:T(8,128)} copy(f32[59,1024]{1,0:T(8,128)} %get-tuple-element.5) | data formatting | bytes 483328
